TPU v7x, 512 devices: a whole 4x4x16 slice. The times are simulated.
512 devices in a mesh: dp: 32 (over z, x_hi), lon: 16 (over y, x_lo, core).
Axes of the slice: x: 4 (x_hi: 2, x_lo: 2; x = x_hi * 2 + x_lo), y: 4, z: 16, core: 2. Of those that a mesh axis runs over, the one named last changes fastest.
Arguments:
- fields: bfloat16 [32, 128, 48, 768], P('dp', 'lon'), may hold values from -6 to 6
- cotangent: bfloat16 [32, 128, 48, 768], P('dp', 'lon'), may hold values from -6 to 6
- first_weight: bfloat16 [2, 8, 96, 96], replicated, may hold values from -0.4375 to 0.4375
- second_weight: bfloat16 [2, 8, 96, 96], replicated, may hold values from -0.4375 to 0.4375
Outputs:
- layer_out: bfloat16 [32, 128, 48, 768], P('dp', 'lon')
- field_grad: bfloat16 [32, 128, 48, 768], P('dp', 'lon')
- first_grad: float32 [2, 8, 96, 96], replicated
- second_grad: float32 [2, 8, 96, 96], replicated
All inputs are finite; a program needn't handle non-finite values.
Results may differ from a plain program's by a relative error of at most 0.015.
Values may be sent and summed in bfloat16 or wider, within the bound.
A program may use at most 64 MiB of HBM per device.

v0:
```python
import math
import jax
import jax.numpy as jnp
from jax import lax
from jax.sharding import PartitionSpec as P

COEF = 0.7978845608028654
CUBIC = 0.044715


def gelu_value(inner):
    hyper = jnp.tanh(COEF * (inner + CUBIC * inner * inner * inner))
    return 0.5 * inner * (1.0 + hyper)


def gelu_slope(inner):
    hyper = jnp.tanh(COEF * (inner + CUBIC * inner * inner * inner))
    return 0.5 * (1.0 + hyper) + 0.5 * inner * (1.0 - hyper * hyper) * COEF * (
        1.0 + 3.0 * CUBIC * inner * inner
    )


def make_basis(length, count):
    cell_idx = jnp.arange(length, dtype=jnp.int32)
    mode_idx = jnp.arange(count, dtype=jnp.int32)
    product = cell_idx[:, None] * mode_idx[None, :] % length
    angle = product.astype(jnp.float32) * jnp.float32(2.0 * math.pi / length)
    return jnp.stack([jnp.cos(angle), -jnp.sin(angle)], axis=-1).astype(jnp.bfloat16)


def lat_apply(spec, table, lat_scale):
    return (
        jnp.einsum("kphc,phqj->kqjc", spec, table, preferred_element_type=jnp.float32) * lat_scale
    ).astype(jnp.bfloat16)


def forward_weight(weight):
    return jnp.stack([jnp.stack([weight[0], weight[1]]), jnp.stack([-weight[1], weight[0]])])


def adjoint_weight(weight):
    return jnp.stack([jnp.stack([weight[0], -weight[1]]), jnp.stack([weight[1], weight[0]])])


def block_product(spec, stacked):
    return jnp.einsum("kphbi,pqbij->kqhbj", spec, stacked, preferred_element_type=jnp.float32)


def block_adjoint(spec, stacked):
    return jnp.einsum("kphbj,pqbij->kqhbi", spec, stacked, preferred_element_type=jnp.float32)


def block_outer(left, right):
    pairs = jnp.einsum("kphbi,kqhbj->pqbij", left, right, preferred_element_type=jnp.float32)
    return jnp.stack([pairs[0, 0] + pairs[1, 1], pairs[0, 1] - pairs[1, 0]])


def on_device(fields, cotangent, first_weight, second_weight):
    cell_rows = fields[0]
    cot_rows = cotangent[0]
    lat_rows = cell_rows.shape[1]
    channels = cell_rows.shape[2]
    groups = first_weight.shape[1]
    group_width = first_weight.shape[2]
    lon_count = lax.axis_size("lon")
    total_cells = cell_rows.shape[0] * lon_count
    dft_basis = make_basis(total_cells, total_cells // 2)
    lat_basis = make_basis(lat_rows, lat_rows)
    cos_tab = lat_basis[:, :, 0]
    sin_tab = lat_basis[:, :, 1]
    lat_fwd_table = jnp.stack(
        [jnp.stack([cos_tab, sin_tab], axis=1), jnp.stack([-sin_tab, cos_tab], axis=1)], axis=0
    )
    lat_inv_table = jnp.stack(
        [jnp.stack([cos_tab.T, -sin_tab.T], axis=1), jnp.stack([sin_tab.T, cos_tab.T], axis=1)],
        axis=0,
    )
    norm_scale = 1.0 / math.sqrt(total_cells)
    lat_scale = 1.0 / math.sqrt(lat_rows)
    local_modes = cell_rows.shape[0] // 2
    mode_idx = lax.axis_index("lon") * local_modes + jnp.arange(local_modes, dtype=jnp.int32)
    mode_weight = jnp.where(mode_idx == 0, 1.0, 2.0).astype(jnp.bfloat16)[:, None, None, None]
    first_fwd = forward_weight(first_weight)
    second_fwd = forward_weight(second_weight)
    first_adj = adjoint_weight(first_weight)
    second_adj = adjoint_weight(second_weight)

    def local_dft(all_lines):
        return (
            jnp.einsum("whc,wkp->kphc", all_lines, dft_basis, preferred_element_type=jnp.float32)
            * norm_scale
        ).astype(jnp.bfloat16)

    def local_idft(all_modes):
        return (
            jnp.einsum("kphc,wkp->whc", all_modes, dft_basis, preferred_element_type=jnp.float32)
            * norm_scale
        ).astype(jnp.bfloat16)

    def lines_to_modes(all_lines):
        return lax.all_to_all(local_dft(all_lines), "lon", split_axis=0, concat_axis=3, tiled=True)

    def modes_to_lines(all_modes):
        return lax.all_to_all(local_idft(all_modes), "lon", split_axis=0, concat_axis=2, tiled=True)

    def to_spectrum(grid_rows):
        return lines_to_modes(
            lax.all_to_all(grid_rows, "lon", split_axis=2, concat_axis=0, tiled=True)
        )

    def to_cells(spec_rows):
        return modes_to_lines(
            lax.all_to_all(spec_rows, "lon", split_axis=3, concat_axis=0, tiled=True)
        )

    def split_groups(spec_rows):
        return spec_rows.reshape(local_modes, 2, lat_rows, groups, group_width)

    def join_groups(spec_rows):
        return spec_rows.astype(jnp.bfloat16).reshape(local_modes, 2, lat_rows, channels)

    lon_spec = to_spectrum(cell_rows)
    spectrum = split_groups(lat_apply(lon_spec, lat_fwd_table, lat_scale))
    inner = block_product(spectrum, first_fwd)
    act = gelu_value(inner).astype(jnp.bfloat16)
    mixed = join_groups(block_product(act, second_fwd)) * mode_weight
    mixed_lon = lat_apply(mixed, lat_inv_table, lat_scale)
    wave = to_cells(mixed_lon)
    dual_lon = to_spectrum(cot_rows)
    dual = split_groups(lat_apply(dual_lon, lat_fwd_table, lat_scale) * mode_weight)
    back = block_adjoint(dual, second_adj)
    pre = (back * gelu_slope(inner)).astype(jnp.bfloat16)
    back_spec = join_groups(block_adjoint(pre, first_adj))
    back_lon = lat_apply(back_spec, lat_inv_table, lat_scale)
    pull = to_cells(back_lon)
    layer_out = (cell_rows.astype(jnp.float32) + wave.astype(jnp.float32)).astype(jnp.bfloat16)
    field_grad = (cot_rows.astype(jnp.float32) + pull.astype(jnp.float32)).astype(jnp.bfloat16)
    sample_count = lax.axis_size("dp")
    second_term = block_outer(act, dual) / sample_count
    first_term = block_outer(spectrum, pre) / sample_count
    first_grad, second_grad = lax.psum((first_term, second_term), ("dp", "lon"))
    return (layer_out[None], field_grad[None], first_grad, second_grad)


def solution(mesh):
    placed = (P("dp", "lon", None, None), P("dp", "lon", None, None), P(), P())
    return jax.shard_map(
        on_device,
        mesh=mesh,
        in_specs=placed,
        out_specs=(P("dp", "lon", None, None), P("dp", "lon", None, None), P(), P()),
        check_vma=False,
    )
```

profile of v0, /device:TPU:1, one launch (start us, length us, event | category | flops | bytes accessed | tf_op | source)
XLA Modules:
  0.0 643.6 jit_solution(1187848861176454927)
XLA Ops:
  7.2 2.0 copy.123
  9.3 3.1 reshape.309
  12.4 11.0 %all-to-all-start = ((bf16[16,2,9216]{2,1,0:T(2,128)(2,1)}), bf16[16,2,9216]{2,1,0:T(2,128)(2,1)}, u32[]{:S(2)}, u32[]{:S(2)}) async-start(bf16[16,2,9216]{2,1,0:T(2,128)(2,1)} %reshape.309), calls=%async_computation | async-start | bytes 1179648 | tf_op jit(solution)/shard_map/all_to_all | solution.py:108
  24.6 3.1 reshape.317
  30.0 4.0 all-to-all-done
  34.1 5.2 all-to-all-start.4
  40.8 2.4 reshape.310
  45.8 1.4 copy.126
  47.2 3.1 reshape.311
  50.3 6.4 %all-to-all-start.1 = ((bf16[16,2,9216]{2,1,0:T(2,128)(2,1)}), bf16[16,2,9216]{2,1,0:T(2,128)(2,1)}, u32[]{:S(2)}, u32[]{:S(2)}) async-start(bf16[16,2,9216]{2,1,0:T(2,128)(2,1)} %reshape.311), calls=%async_computation.1 | async-start | bytes 1179648 | tf_op jit(solution)/shard_map/all_to_all | solution.py:101
  59.0 2.4 reshape.318
  64.0 1.4 copy.140
  65.4 3.1 reshape.319
  68.5 5.9 all-to-all-start.5
  77.1 2.4 reshape.312
  80.6 1.6 reshape.275
  83.4 1.6 all-to-all-done.5
  85.0 2.4 reshape.320
  87.5 2.2 copy.141
  89.7 2.9 reshape.288
  94.9 1.6 convolution_bitcast_fusion
  101.3 3.1 reshape.321
  104.4 4.5 all-to-all-start.6
  108.9 1.7 fusion.37
  113.5 2.2 copy.132
  115.7 4.1 reshape.313
  119.9 1.4 fusion.69
  121.4 5.8 all-to-all-start.2
  129.2 1.8 reshape.322
  132.3 1.5 fusion.30
  133.8 1.8 copy.151
  135.6 3.1 reshape.323
  138.7 5.7 all-to-all-start.7
  144.4 2.4 reshape.314
  148.1 1.5 fusion.27
  149.6 1.8 copy.135
  151.4 3.1 reshape.315
  154.5 451.1 %all-reduce.3.cloned.1.call-done = (f32[2,8,96,96]{2,3,1,0:T(8,128)}, f32[2,8,96,96]{2,3,1,0:T(8,128)}) async-done(((f32[2,8,96,96]{2,3,1,0:T(8,128)}, f32[2,8,96,96]{2,3,1,0:T(8,128)}), (f32[2,8,96,96]{2,3,1,0:T(8,128)}, f32[2,8,96,96]{2,3,1,0:T(8,128)})) %all-reduce.3.cloned.1.call-update) | async-done | bytes 1179664 | tf_op jit(solution)/shard_map/psum | solution.py:141
  605.7 2.4 copy.158
  609.2 7.4 %all-to-all-start.3 = ((bf16[16,2,9216]{2,1,0:T(2,128)(2,1)}), bf16[16,2,9216]{2,1,0:T(2,128)(2,1)}, u32[]{:S(2)}, u32[]{:S(2)}) async-start(bf16[16,2,9216]{2,1,0:T(2,128)(2,1)} %reshape.315), calls=%async_computation.3 | async-start | bytes 1179648 | tf_op jit(solution)/shard_map/all_to_all | solution.py:104
  616.6 2.4 reshape.324
  619.4 1.8 copy.152
  621.2 2.2 reshape.269
  623.5 2.3 add_convert_fusion
  627.1 2.4 reshape.316
  629.9 1.8 copy.136
  631.7 2.2 reshape.268
  634.0 2.3 add_convert_fusion.1
  (123 shorter events, 34.8 us)
Async XLA Ops:
  12.3 11.0 %copy-start = (bf16[1,8,48,768]{3,2,1,0:T(8,128)(2,1)S(1)}, bf16[1,8,48,768]{3,2,1,0:T(8,128)(2,1)}, u32[]{:S(2)}) copy-start(bf16[1,8,48,768]{3,2,1,0:T(8,128)(2,1)} %param.5) | copy-start | bytes 1769476
  12.4 21.7 %all-to-all-start = ((bf16[16,2,9216]{2,1,0:T(2,128)(2,1)}), bf16[16,2,9216]{2,1,0:T(2,128)(2,1)}, u32[]{:S(2)}, u32[]{:S(2)}) async-start(bf16[16,2,9216]{2,1,0:T(2,128)(2,1)} %reshape.309), calls=%async_computation | async-start | bytes 1179648 | tf_op jit(solution)/shard_map/all_to_all | solution.py:108
  24.6 15.4 %copy-start.21 = (bf16[2,8,96,96]{3,2,1,0:T(8,128)(2,1)S(1)}, bf16[2,8,96,96]{3,2,1,0:T(8,128)(2,1)}, u32[]{:S(2)}) copy-start(bf16[2,8,96,96]{3,2,1,0:T(8,128)(2,1)} %param.6) | copy-start | bytes 884740
  34.1 16.2 %all-to-all-start.4 = ((bf16[16,2,9216]{2,1,0:T(2,128)(2,1)}), bf16[16,2,9216]{2,1,0:T(2,128)(2,1)}, u32[]{:S(2)}, u32[]{:S(2)}) async-start(bf16[16,2,9216]{2,1,0:T(2,128)(2,1)} %reshape.317), calls=%async_computation.4 | async-start | bytes 1179648 | tf_op jit(solution)/shard_map/all_to_all | solution.py:108
  44.3 1.0 copy-start.14
  47.2 9.6 %copy-start.29 = (bf16[48,1,48]{2,0,1:T(8,128)(2,1)S(1)}, bf16[48,1,48]{2,0,1:T(8,128)(2,1)}, u32[]{:S(2)}) copy-start(bf16[48,1,48]{2,0,1:T(8,128)(2,1)} %get-tuple-element.48) | copy-start | bytes 13828
  47.2 9.6 %copy-start.30 = (bf16[48,1,48]{2,0,1:T(8,128)(2,1)S(1)}, bf16[48,1,48]{2,0,1:T(8,128)(2,1)}, u32[]{:S(2)}) copy-start(bf16[48,1,48]{2,0,1:T(8,128)(2,1)} %get-tuple-element.49) | copy-start | bytes 13828
  47.2 9.6 %copy-start.31 = (bf16[48,1,48]{2,0,1:T(8,128)(2,1)S(1)}, bf16[48,1,48]{2,0,1:T(8,128)(2,1)}, u32[]{:S(2)}) copy-start(bf16[48,1,48]{2,0,1:T(8,128)(2,1)} %fusion.91) | copy-start | bytes 13828
  47.2 10.2 %copy-start.22 = (bf16[2,8,96,96]{3,2,1,0:T(8,128)(2,1)S(1)}, bf16[2,8,96,96]{3,2,1,0:T(8,128)(2,1)}, u32[]{:S(2)}) copy-start(bf16[2,8,96,96]{3,2,1,0:T(8,128)(2,1)} %param.7) | copy-start | bytes 884740
  50.3 18.2 %all-to-all-start.1 = ((bf16[16,2,9216]{2,1,0:T(2,128)(2,1)}), bf16[16,2,9216]{2,1,0:T(2,128)(2,1)}, u32[]{:S(2)}, u32[]{:S(2)}) async-start(bf16[16,2,9216]{2,1,0:T(2,128)(2,1)} %reshape.311), calls=%async_computation.1 | async-start | bytes 1179648 | tf_op jit(solution)/shard_map/all_to_all | solution.py:101
  57.5 0.7 copy-start.2
  62.5 1.0 copy-start.15
  65.4 9.5 %copy-start.8 = (bf16[1,8,96,96]{3,2,0,1:T(8,128)(2,1)S(1)}, bf16[1,8,96,96]{3,2,0,1:T(8,128)(2,1)}, u32[]{:S(2)}) copy-start(bf16[1,8,96,96]{3,2,0,1:T(8,128)(2,1)} %get-tuple-element.26) | copy-start | bytes 442372
  65.4 9.5 %copy-start.9 = (bf16[1,8,96,96]{3,2,0,1:T(8,128)(2,1)S(1)}, bf16[1,8,96,96]{3,2,0,1:T(8,128)(2,1)}, u32[]{:S(2)}) copy-start(bf16[1,8,96,96]{3,2,0,1:T(8,128)(2,1)} %get-tuple-element.27) | copy-start | bytes 442372
  65.4 9.5 %copy-start.10 = (bf16[1,8,96,96]{3,2,0,1:T(8,128)(2,1)S(1)}, bf16[1,8,96,96]{3,2,0,1:T(8,128)(2,1)}, u32[]{:S(2)}) copy-start(bf16[1,8,96,96]{3,2,0,1:T(8,128)(2,1)} %get-tuple-element.28) | copy-start | bytes 442372
  68.5 7.5 %copy-start.11 = (bf16[1,8,96,96]{3,2,0,1:T(8,128)(2,1)S(1)}, bf16[1,8,96,96]{3,2,0,1:T(8,128)(2,1)}, u32[]{:S(2)}) copy-start(bf16[1,8,96,96]{3,2,0,1:T(8,128)(2,1)} %get-tuple-element.31) | copy-start | bytes 442372
  68.5 7.5 %copy-start.12 = (bf16[1,8,96,96]{3,2,0,1:T(8,128)(2,1)S(1)}, bf16[1,8,96,96]{3,2,0,1:T(8,128)(2,1)}, u32[]{:S(2)}) copy-start(bf16[1,8,96,96]{3,2,0,1:T(8,128)(2,1)} %get-tuple-element.32) | copy-start | bytes 442372
  68.5 7.5 %copy-start.13 = (bf16[1,8,96,96]{3,2,0,1:T(8,128)(2,1)S(1)}, bf16[1,8,96,96]{3,2,0,1:T(8,128)(2,1)}, u32[]{:S(2)}) copy-start(bf16[1,8,96,96]{3,2,0,1:T(8,128)(2,1)} %get-tuple-element.33) | copy-start | bytes 442372
  68.5 16.5 %all-to-all-start.5 = ((bf16[16,2,9216]{2,1,0:T(2,128)(2,1)}), bf16[16,2,9216]{2,1,0:T(2,128)(2,1)}, u32[]{:S(2)}, u32[]{:S(2)}) async-start(bf16[16,2,9216]{2,1,0:T(2,128)(2,1)} %reshape.319), calls=%async_computation.5 | async-start | bytes 1179648 | tf_op jit(solution)/shard_map/all_to_all | solution.py:101
  80.6 1.6 copy-start.25
  80.6 1.6 copy-start.27
  89.7 2.9 copy-start.26
  89.7 2.9 copy-start.28
  89.7 2.9 copy-start.32
  92.6 1.2 copy-start.1
  94.8 1.7 copy-start.7
  94.8 1.7 copy-start.19
  94.8 1.6 copy-start.20
  96.5 1.3 copy-start.17
  96.5 1.3 copy-start.18
  97.8 0.9 copy-start.5
  98.7 1.2 copy-start.23
  98.7 1.2 copy-start.24
  101.3 7.6 %copy-start.3 = (bf16[2,8,96,96]{3,2,0,1:T(8,128)(2,1)S(1)}, bf16[2,8,96,96]{3,2,0,1:T(8,128)(2,1)}, u32[]{:S(2)}) copy-start(bf16[2,8,96,96]{3,2,0,1:T(8,128)(2,1)} %copy-done.2) | copy-start | bytes 884740
  104.4 17.0 %all-to-all-start.6 = ((bf16[16,2,9216]{2,1,0:T(2,128)(2,1)}), bf16[16,2,9216]{2,1,0:T(2,128)(2,1)S(1)}, u32[]{:S(2)}, u32[]{:S(2)}) async-start(bf16[16,2,9216]{2,1,0:T(2,128)(2,1)} %reshape.321), calls=%async_computation.6 | async-start | bytes 1179648 | tf_op jit(solution)/shard_map/all_to_all | solution.py:113
  111.8 1.2 copy-start.6
  121.4 17.3 %all-to-all-start.2 = ((bf16[16,2,9216]{2,1,0:T(2,128)(2,1)}), bf16[16,2,9216]{2,1,0:T(2,128)(2,1)}, u32[]{:S(2)}, u32[]{:S(2)}) async-start(bf16[16,2,9216]{2,1,0:T(2,128)(2,1)} %reshape.313), calls=%async_computation.2 | async-start | bytes 1179648 | tf_op jit(solution)/shard_map/all_to_all | solution.py:113
  127.2 478.5 %all-reduce.3.cloned.1.call-start = ((), (), s32[]{:S(2)}) async-start(), calls=%async_computation.8 | async-start | bytes 3145728 | tf_op jit(solution)/shard_map/psum | solution.py:141
  131.0 1.2 copy-start.16
  138.7 470.5 %all-to-all-start.7 = ((bf16[16,2,9216]{2,1,0:T(2,128)(2,1)}), bf16[16,2,9216]{2,1,0:T(2,128)(2,1)}, u32[]{:S(2)}, u32[]{:S(2)}) async-start(bf16[16,2,9216]{2,1,0:T(2,128)(2,1)} %reshape.323), calls=%async_computation.7 | async-start | bytes 1179648 | tf_op jit(solution)/shard_map/all_to_all | solution.py:104
  605.7 2.4 copy-start.4
  609.2 17.9 %all-to-all-start.3 = ((bf16[16,2,9216]{2,1,0:T(2,128)(2,1)}), bf16[16,2,9216]{2,1,0:T(2,128)(2,1)}, u32[]{:S(2)}, u32[]{:S(2)}) async-start(bf16[16,2,9216]{2,1,0:T(2,128)(2,1)} %reshape.315), calls=%async_computation.3 | async-start | bytes 1179648 | tf_op jit(solution)/shard_map/all_to_all | solution.py:104
Sparse Core Ops, SparseCore 0:
  133.9 471.6 all-reduce.2
where the time goes:
time: 652 us; the launch traced here: 644 us
  waiting for transfers between devices  458 us (70%)
  local copies, waits for them, and re-layouts  88.6 us (14%)
  starting transfers between devices  52 us (8%)
  other arithmetic  17.4 us (3%)
  between operations  15.2 us (2%)
  matrix products  12.2 us (2%)
    psum x1, waiting for transfers between devices, on_device(): first_grad, second_grad = lax.psum((first_term, second_term), ('dp', 'lon'))  451 us
    unnamed x90, local copies, waits for them, and re-layouts  52.7 us
    all_to_all x2, starting transfers between devices, to_spectrum(): lax.all_to_all(grid_rows, 'lon', split_axis=2, concat_axis=0, tiled=True)  16.1 us
    all_to_all x2, starting transfers between devices, modes_to_lines(): lax.all_to_all(local_idft(all_modes), 'lon', split_axis=0, concat_axis=2,...  13.2 us
  transfers between devices with their start and end apart: 9, of which 4 were waited for; matrix products, arithmetic and copies ran while one was open for 13% of the time, Pallas kernels for 0%

commit v1 on v0

--- a/solution.py
+++ b/solution.py
@@ -6,6 +6,13 @@
 
 COEF = 0.7978845608028654
 CUBIC = 0.044715
+
+
+def swap_blocks(x, mesh_axis, split, join):
+    peers = lax.axis_size(mesh_axis)
+    tiles = jnp.stack(jnp.split(x, peers, axis=split), axis=0)
+    tiles = lax.all_to_all(tiles, mesh_axis, split_axis=0, concat_axis=0)
+    return jnp.concatenate(tiles, axis=join)
 
 
 def gelu_value(inner):
@@ -98,7 +105,7 @@
         ).astype(jnp.bfloat16)
 
     def lines_to_modes(all_lines):
-        return lax.all_to_all(local_dft(all_lines), "lon", split_axis=0, concat_axis=3, tiled=True)
+        return swap_blocks(local_dft(all_lines), "lon", 0, 3)
 
     def modes_to_lines(all_modes):
         return lax.all_to_all(local_idft(all_modes), "lon", split_axis=0, concat_axis=2, tiled=True)

time: 652 us -> 762 us (1.17)
  local copies, waits for them, and re-layouts: 88.6 us -> 204 us
    another operation x0 -> x36, local copies, waits for them, and re-layouts: none -> 92.1 us  [swap_blocks(): tiles = jnp.stack(jnp.split(x, peers, axis=split), axis=0)]
    unnamed x90 -> x162, local copies, waits for them, and re-layouts: 52.7 us -> 79.9 us
    all_to_all x4 -> x0, local copies, waits for them, and re-layouts: 7.68 us -> none  [lines_to_modes(): lax.all_to_all(local_dft(all_lines), 'lon', split_axis=0, concat_axis=3,...]
  transfers between devices with their start and end apart: 9 -> 9, of which waited for: 4 -> 4; matrix products, arithmetic and copies ran while one was open for 13% -> 26% of each run, Pallas kernels for 0% -> 0%
where the time goes in v1:
time: 762 us; the launch traced here: 755 us
  waiting for transfers between devices  456 us (60%)
  local copies, waits for them, and re-layouts  204 us (27%)
  starting transfers between devices  52.6 us (7%)
  other arithmetic  15.7 us (2%)
  between operations  15.4 us (2%)
  matrix products  12.2 us (2%)
    psum x1, waiting for transfers between devices, on_device(): first_grad, second_grad = lax.psum((first_term, second_term), ('dp', 'lon'))  451 us
    another operation x36, local copies, waits for them, and re-layouts, swap_blocks(): tiles = jnp.stack(jnp.split(x, peers, axis=split), axis=0)  92.1 us
    unnamed x162, local copies, waits for them, and re-layouts  79.9 us
    all_to_all x2, starting transfers between devices, to_spectrum(): lax.all_to_all(grid_rows, 'lon', split_axis=2, concat_axis=0, tiled=True)  16.5 us
  transfers between devices with their start and end apart: 9, of which 4 were waited for; matrix products, arithmetic and copies ran while one was open for 26% of the time, Pallas kernels for 0%

profile of v1, /device:TPU:1, one launch (start us, length us, event | category | flops | bytes accessed | tf_op | source)
XLA Modules:
  0.0 755.3 jit_solution(17666405755317642792)
XLA Ops:
  9.3 3.1 reshape.333
  12.4 11.0 %all-to-all-start.4 = ((bf16[16,2,9216]{2,1,0:T(2,128)(2,1)}), bf16[16,2,9216]{2,1,0:T(2,128)(2,1)}, u32[]{:S(2)}, u32[]{:S(2)}) async-start(bf16[16,2,9216]{2,1,0:T(2,128)(2,1)} %reshape.333), calls=%async_computation.4 | async-start | bytes 1179648 | tf_op jit(solution)/shard_map/all_to_all | solution.py:115
  25.1 3.1 reshape.325
  31.5 2.6 all-to-all-done.4
  34.1 5.5 all-to-all-start
  44.6 7.9 %slice_bitcast_fusion = (bf16[1,4,2,48,48]{1,4,3,2,0:T(8,128)(2,1)S(1)}, bf16[1,4,2,48,48]{1,4,3,2,0:T(8,128)(2,1)S(1)}, bf16[1,4,2,48,48]{1,4,3,2,0:T(8,128)(2,...) fusion(bf16[64,2,48,48]{0,3,2,1:T(8,128)(2,1)S(1)} %multiply_co, ...), kind=kLoop, calls=%fused_computation.48 | loop fusion | bytes 1179648 | tf_op jit(solution)/shard_map/stack | solution.py:13
  52.5 2.7 copy.149
  56.7 2.7 copy.150
  59.3 2.7 copy.151
  62.0 2.7 copy.152
  64.7 2.7 copy.153
  67.3 2.7 copy.154
  70.0 2.7 copy.155
  72.6 2.7 copy.156
  75.3 2.7 copy.157
  78.0 2.7 copy.158
  80.6 2.7 copy.159
  83.3 2.7 copy.160
  85.9 2.7 copy.161
  103.1 4.1 reshape.335
  107.3 6.3 all-to-all-start.5
  113.6 2.4 reshape.326
  118.6 7.9 %slice_bitcast_fusion.16 = (bf16[1,4,2,48,48]{1,4,3,2,0:T(8,128)(2,1)S(1)}, bf16[1,4,2,48,48]{1,4,3,2,0:T(8,128)(2,1)S(1)}, bf16[1,4,2,48,48]{1,4,3,2,0:T(8,128)...) fusion(bf16[64,2,48,48]{0,3,2,1:T(8,128)(2,1)S(1)} %multiply_co, ...), kind=kLoop, calls=%fused_computation.64 | loop fusion | bytes 1179648 | tf_op jit(solution)/shard_map/stack | solution.py:13
  126.5 2.7 copy.120
  130.7 2.7 copy.121
  133.4 2.7 copy.122
  136.0 2.7 copy.123
  138.7 2.7 copy.124
  141.3 2.7 copy.125
  144.0 2.7 copy.126
  146.7 2.7 copy.127
  149.3 2.7 copy.128
  152.0 2.7 copy.129
  154.7 2.7 copy.130
  157.3 2.7 copy.131
  160.0 2.7 copy.132
  177.2 4.4 reshape.327
  181.6 5.9 all-to-all-start.1
  212.6 3.1 reshape.337
  215.7 5.0 all-to-all-start.6
  227.5 4.1 reshape.329
  233.1 5.7 all-to-all-start.2
  247.3 3.1 reshape.339
  250.4 5.7 all-to-all-start.7
  263.2 3.1 reshape.331
  266.2 451.0 %all-reduce.3.cloned.1.call-done = (f32[2,8,96,96]{2,3,1,0:T(8,128)}, f32[2,8,96,96]{2,3,1,0:T(8,128)}) async-done(((f32[2,8,96,96]{2,3,1,0:T(8,128)}, f32[2,8,96,96]{2,3,1,0:T(8,128)}), (f32[2,8,96,96]{2,3,1,0:T(8,128)}, f32[2,8,96,96]{2,3,1,0:T(8,128)})) %all-reduce.3.cloned.1.call-update) | async-done | bytes 1179664 | tf_op jit(solution)/shard_map/psum | solution.py:148
  720.8 7.5 all-to-all-start.3
  728.3 2.4 reshape.340
  (229 shorter events, 115.7 us)
Async XLA Ops:
  12.3 11.5 %copy-start.2 = (bf16[1,8,48,768]{3,2,1,0:T(8,128)(2,1)S(1)}, bf16[1,8,48,768]{3,2,1,0:T(8,128)(2,1)}, u32[]{:S(2)}) copy-start(bf16[1,8,48,768]{3,2,1,0:T(8,128)(2,1)} %param.4) | copy-start | bytes 1769476
  12.4 21.7 %all-to-all-start.4 = ((bf16[16,2,9216]{2,1,0:T(2,128)(2,1)}), bf16[16,2,9216]{2,1,0:T(2,128)(2,1)}, u32[]{:S(2)}, u32[]{:S(2)}) async-start(bf16[16,2,9216]{2,1,0:T(2,128)(2,1)} %reshape.333), calls=%async_computation.4 | async-start | bytes 1179648 | tf_op jit(solution)/shard_map/all_to_all | solution.py:115
  25.1 3.1 copy-start.23
  25.1 3.1 copy-start.24
  28.2 5.9 copy-start
  28.3 5.8 copy-start.3
  29.8 14.3 %copy-start.16 = (bf16[128,64,1]{0,1,2:T(8,128)(2,1)}, bf16[128,64,1]{0,1,2:T(8,128)(2,1)S(1)}, u32[]{:S(2)}) copy-start(bf16[128,64,1]{0,1,2:T(8,128)(2,1)S(1)} %get-tuple-element.77) | copy-start | bytes 49156
  34.1 73.2 %all-to-all-start = ((bf16[16,2,9216]{2,1,0:T(2,128)(2,1)}), bf16[16,2,9216]{2,1,0:T(2,128)(2,1)}, u32[]{:S(2)}, u32[]{:S(2)}) async-start(bf16[16,2,9216]{2,1,0:T(2,128)(2,1)} %reshape.325), calls=%async_computation | async-start | bytes 1179648 | tf_op jit(solution)/shard_map/all_to_all | solution.py:115
  90.0 5.3 copy-start.43
  90.0 6.0 copy-start.41
  90.0 6.6 copy-start.39
  90.0 7.3 copy-start.37
  90.8 3.9 copy-start.45
  90.8 7.2 copy-start.35
  90.8 7.8 %copy-start.33 = (bf16[1,4,2,48,48]{4,3,2,1,0:T(8,128)(2,1)S(1)}, bf16[1,4,2,48,48]{4,3,2,1,0:T(8,128)(2,1)}, u32[]{:S(2)}) copy-start(bf16[1,4,2,48,48]{4,3,2,1,0:T(8,128)(2,1)} %copy.158) | copy-start | bytes 110596
  90.8 8.5 %copy-start.31 = (bf16[1,4,2,48,48]{4,3,2,1,0:T(8,128)(2,1)S(1)}, bf16[1,4,2,48,48]{4,3,2,1,0:T(8,128)(2,1)}, u32[]{:S(2)}) copy-start(bf16[1,4,2,48,48]{4,3,2,1,0:T(8,128)(2,1)} %copy.159) | copy-start | bytes 110596
  90.8 9.1 %copy-start.29 = (bf16[1,4,2,48,48]{4,3,2,1,0:T(8,128)(2,1)S(1)}, bf16[1,4,2,48,48]{4,3,2,1,0:T(8,128)(2,1)}, u32[]{:S(2)}) copy-start(bf16[1,4,2,48,48]{4,3,2,1,0:T(8,128)(2,1)} %copy.160) | copy-start | bytes 110596
  90.8 9.7 %copy-start.27 = (bf16[1,4,2,48,48]{4,3,2,1,0:T(8,128)(2,1)S(1)}, bf16[1,4,2,48,48]{4,3,2,1,0:T(8,128)(2,1)}, u32[]{:S(2)}) copy-start(bf16[1,4,2,48,48]{4,3,2,1,0:T(8,128)(2,1)} %copy.161) | copy-start | bytes 110596
  90.8 10.4 %copy-start.25 = (bf16[1,4,2,48,48]{4,3,2,1,0:T(8,128)(2,1)S(1)}, bf16[1,4,2,48,48]{4,3,2,1,0:T(8,128)(2,1)}, u32[]{:S(2)}) copy-start(bf16[1,4,2,48,48]{4,3,2,1,0:T(8,128)(2,1)} %copy.162) | copy-start | bytes 110596
  107.3 74.3 %all-to-all-start.5 = ((bf16[16,2,9216]{2,1,0:T(2,128)(2,1)}), bf16[16,2,9216]{2,1,0:T(2,128)(2,1)}, u32[]{:S(2)}, u32[]{:S(2)}) async-start(bf16[16,2,9216]{2,1,0:T(2,128)(2,1)} %reshape.335), calls=%async_computation.5 | async-start | bytes 1179648 | tf_op jit(solution)/shard_map/all_to_all | solution.py:14
  164.1 5.3 copy-start.44
  164.1 6.0 copy-start.42
  164.1 6.6 copy-start.40
  164.1 7.3 copy-start.38
  164.8 3.9 copy-start.46
  164.9 7.2 copy-start.36
  164.9 7.8 %copy-start.34 = (bf16[1,4,2,48,48]{4,3,2,1,0:T(8,128)(2,1)S(1)}, bf16[1,4,2,48,48]{4,3,2,1,0:T(8,128)(2,1)}, u32[]{:S(2)}) copy-start(bf16[1,4,2,48,48]{4,3,2,1,0:T(8,128)(2,1)} %copy.129) | copy-start | bytes 110596
  164.9 8.5 %copy-start.32 = (bf16[1,4,2,48,48]{4,3,2,1,0:T(8,128)(2,1)S(1)}, bf16[1,4,2,48,48]{4,3,2,1,0:T(8,128)(2,1)}, u32[]{:S(2)}) copy-start(bf16[1,4,2,48,48]{4,3,2,1,0:T(8,128)(2,1)} %copy.130) | copy-start | bytes 110596
  164.9 9.1 %copy-start.30 = (bf16[1,4,2,48,48]{4,3,2,1,0:T(8,128)(2,1)S(1)}, bf16[1,4,2,48,48]{4,3,2,1,0:T(8,128)(2,1)}, u32[]{:S(2)}) copy-start(bf16[1,4,2,48,48]{4,3,2,1,0:T(8,128)(2,1)} %copy.131) | copy-start | bytes 110596
  164.9 9.7 %copy-start.28 = (bf16[1,4,2,48,48]{4,3,2,1,0:T(8,128)(2,1)S(1)}, bf16[1,4,2,48,48]{4,3,2,1,0:T(8,128)(2,1)}, u32[]{:S(2)}) copy-start(bf16[1,4,2,48,48]{4,3,2,1,0:T(8,128)(2,1)} %copy.132) | copy-start | bytes 110596
  164.9 10.4 %copy-start.26 = (bf16[1,4,2,48,48]{4,3,2,1,0:T(8,128)(2,1)S(1)}, bf16[1,4,2,48,48]{4,3,2,1,0:T(8,128)(2,1)}, u32[]{:S(2)}) copy-start(bf16[1,4,2,48,48]{4,3,2,1,0:T(8,128)(2,1)} %copy.133) | copy-start | bytes 110596
  177.2 10.9 %copy-start.13 = (bf16[1,8,96,96]{3,2,0,1:T(8,128)(2,1)S(1)}, bf16[1,8,96,96]{3,2,0,1:T(8,128)(2,1)}, u32[]{:S(2)}) copy-start(bf16[1,8,96,96]{3,2,0,1:T(8,128)(2,1)} %get-tuple-element.58) | copy-start | bytes 442372
  177.2 10.9 %copy-start.14 = (bf16[1,8,96,96]{3,2,0,1:T(8,128)(2,1)S(1)}, bf16[1,8,96,96]{3,2,0,1:T(8,128)(2,1)}, u32[]{:S(2)}) copy-start(bf16[1,8,96,96]{3,2,0,1:T(8,128)(2,1)} %get-tuple-element.59) | copy-start | bytes 442372
  177.2 10.9 %copy-start.15 = (bf16[1,8,96,96]{3,2,0,1:T(8,128)(2,1)S(1)}, bf16[1,8,96,96]{3,2,0,1:T(8,128)(2,1)}, u32[]{:S(2)}) copy-start(bf16[1,8,96,96]{3,2,0,1:T(8,128)(2,1)} %get-tuple-element.60) | copy-start | bytes 442372
  181.6 7.5 copy-start.10
  181.6 7.5 copy-start.11
  181.6 7.5 copy-start.12
  181.6 16.5 %all-to-all-start.1 = ((bf16[16,2,9216]{2,1,0:T(2,128)(2,1)}), bf16[16,2,9216]{2,1,0:T(2,128)(2,1)}, u32[]{:S(2)}, u32[]{:S(2)}) async-start(bf16[16,2,9216]{2,1,0:T(2,128)(2,1)} %reshape.327), calls=%async_computation.1 | async-start | bytes 1179648 | tf_op jit(solution)/shard_map/all_to_all | solution.py:14
  201.6 1.8 copy-start.50
  201.6 1.8 copy-start.52
  205.6 2.2 copy-start.8
  212.6 8.0 %copy-start.4 = (bf16[2,8,96,96]{3,2,0,1:T(8,128)(2,1)S(1)}, bf16[2,8,96,96]{3,2,0,1:T(8,128)(2,1)}, u32[]{:S(2)}) copy-start(bf16[2,8,96,96]{3,2,0,1:T(8,128)(2,1)} %copy-done.3) | copy-start | bytes 884740
  215.7 17.4 %all-to-all-start.6 = ((bf16[16,2,9216]{2,1,0:T(2,128)(2,1)}), bf16[16,2,9216]{2,1,0:T(2,128)(2,1)S(1)}, u32[]{:S(2)}, u32[]{:S(2)}) async-start(bf16[16,2,9216]{2,1,0:T(2,128)(2,1)} %reshape.337), calls=%async_computation.6 | async-start | bytes 1179648 | tf_op jit(solution)/shard_map/all_to_all | solution.py:120
  233.1 17.3 %all-to-all-start.2 = ((bf16[16,2,9216]{2,1,0:T(2,128)(2,1)}), bf16[16,2,9216]{2,1,0:T(2,128)(2,1)}, u32[]{:S(2)}, u32[]{:S(2)}) async-start(bf16[16,2,9216]{2,1,0:T(2,128)(2,1)} %reshape.329), calls=%async_computation.2 | async-start | bytes 1179648 | tf_op jit(solution)/shard_map/all_to_all | solution.py:120
  238.8 478.5 %all-reduce.3.cloned.1.call-start = ((), (), s32[]{:S(2)}) async-start(), calls=%async_computation.8 | async-start | bytes 3145728 | tf_op jit(solution)/shard_map/psum | solution.py:148
  250.4 470.4 %all-to-all-start.7 = ((bf16[16,2,9216]{2,1,0:T(2,128)(2,1)}), bf16[16,2,9216]{2,1,0:T(2,128)(2,1)}, u32[]{:S(2)}, u32[]{:S(2)}) async-start(bf16[16,2,9216]{2,1,0:T(2,128)(2,1)} %reshape.339), calls=%async_computation.7 | async-start | bytes 1179648 | tf_op jit(solution)/shard_map/all_to_all | solution.py:111
  717.3 2.4 copy-start.5
  720.8 18.0 %all-to-all-start.3 = ((bf16[16,2,9216]{2,1,0:T(2,128)(2,1)}), bf16[16,2,9216]{2,1,0:T(2,128)(2,1)}, u32[]{:S(2)}, u32[]{:S(2)}) async-start(bf16[16,2,9216]{2,1,0:T(2,128)(2,1)} %reshape.331), calls=%async_computation.3 | async-start | bytes 1179648 | tf_op jit(solution)/shard_map/all_to_all | solution.py:111
  (15 other events, 19.7 us)
Sparse Core Ops, SparseCore 0:
  245.6 471.6 all-reduce.2
